TPU v7x, 32 devices: a whole 2x2x4 slice. The times are simulated.
32 devices in a mesh: ens: 2 (over x), lon: 16 (over z, y, core).
Axes of the slice: x: 2, y: 2, z: 4, core: 2. Of those that a mesh axis runs over, the one named last changes fastest.
Arguments:
- state: bfloat16 [256, 4, 64, 256], P(('ens', 'lon')), parts along dimension 0, may hold values from -24 to 24
- obs_index: int32 [8192], P(('ens', 'lon')), parts along dimension 0, may hold values from 0 to 511
- obs_value: float32 [8192], P(('ens', 'lon')), parts along dimension 0, may hold values from -20 to 20
- obs_var: float32 [8192], P(('ens', 'lon')), parts along dimension 0, may hold values from 0.5 to 2
Outputs:
- analysis: bfloat16 [256, 4, 64, 256], P(('ens', 'lon')), parts along dimension 0
There are 2 independent parts, one for each index of `ens`. A program takes and returns all parts, laid end to end along the dimension named above; each array names one. Nothing has to cross between parts.
Inputs may be any that keep to these rules, and one draw needn't show every extreme that they name: `obs_index`: a column of the device's own strip.
All inputs are finite; a program needn't handle non-finite values.
Results may differ from a plain program's by a relative error of at most 0.0029.
Values may be sent and summed in bfloat16 or wider, within the bound.
A program may use at most 128 MiB of HBM per device.

v0:
```python
import jax
import jax.numpy as jnp
from jax import lax
from jax.sharding import PartitionSpec as P

REGION = 8
HALO = 4
SWEEPS = 4


EPS = 0.05


def with_halo(cells, sides, width):
    for axis, dim in sides:
        count = lax.axis_size(axis)
        head = lax.slice_in_dim(cells, 0, width, axis=dim)
        tail = lax.slice_in_dim(cells, cells.shape[dim] - width, cells.shape[dim], axis=dim)
        cells = jnp.concatenate(
            [
                lax.ppermute(tail, axis, [(i, (i + 1) % count) for i in range(count)]),
                cells,
                lax.ppermute(head, axis, [((i + 1) % count, i) for i in range(count)]),
            ],
            axis=dim,
        )
    return cells


def taper():
    place = jnp.arange(REGION + 2 * HALO)
    dist = jnp.maximum(0, jnp.maximum(HALO - place, place - (HALO + REGION - 1)))
    line = 1.0 - dist.astype(jnp.float32) / (HALO + 1)
    return line[:, None] * line[None, :]


def windows(block):
    lon_len, nvar, lat_len, members = block.shape
    lon_blocks = lon_len // REGION
    lat_blocks = lat_len // REGION
    split = block.reshape(lon_blocks, REGION, nvar, lat_blocks, REGION, members)
    split = jnp.concatenate([split[:-1], split[1:]], axis=1)
    return jnp.concatenate([split[:, :, :, :-1], split[:, :, :, 1:]], axis=4)


def gram_part(win, lower, upper):
    rho = taper()
    weighted = (win.astype(jnp.float32) * rho[None, lower:upper, None, None, :, None]).astype(
        jnp.bfloat16
    )
    return jnp.einsum("apvbqm,apvbqn->abmn", weighted, win, preferred_element_type=jnp.float32)


def analyse(win, mis_win, scale, gram):
    rho = taper()
    members = win.shape[-1]
    diag = jnp.diagonal(gram, axis1=2, axis2=3)
    cost = (diag[..., :, None] + diag[..., None, :] - 2.0 * gram) / (win.shape[2] * jnp.sum(rho))
    like = scale * jnp.einsum("apxbqm,pq->abm", mis_win, rho, precision=lax.Precision.HIGHEST)
    logw = like - jax.nn.logsumexp(like, axis=-1, keepdims=True)
    pot_g = jnp.zeros(like.shape, jnp.float32)
    pot_f = pot_g
    for sweep in range(SWEEPS):
        pot_f = EPS * logw - EPS * jax.nn.logsumexp((pot_g[..., None, :] - cost) / EPS, axis=-1)
        pot_g = -EPS * jnp.log(1.0 * members) - EPS * jax.nn.logsumexp(
            (pot_f[..., :, None] - cost) / EPS, axis=-2
        )
    transport = (
        members * jnp.exp((pot_f[..., :, None] + pot_g[..., None, :] - cost) / EPS)
    ).astype(jnp.bfloat16)
    own = win[:, HALO : HALO + REGION, :, :, HALO : HALO + REGION, :]
    result = jnp.einsum("apvbqi,abij->apvbqj", own, transport, preferred_element_type=jnp.float32)
    return result.astype(jnp.bfloat16)


def tempering(partial_value, count):
    return count / lax.psum(partial_value, "lon")


def on_device(state, obs_index, obs_value, obs_var):
    lon_dev, nvar, lat, members = state.shape
    nobs_dev = obs_index.shape[0]
    count = nobs_dev * lax.axis_size("lon")
    span = REGION + 2 * HALO
    rows = state[:, 0].reshape(lon_dev * lat, members)
    seen = jnp.take(rows, obs_index, axis=0).astype(jnp.float32)
    centre = jnp.mean(seen, axis=1)
    spread = jnp.sum((seen - centre[:, None]) ** 2, axis=1) / (members - 1)
    partial_value = jnp.sum((obs_value - centre) ** 2 / (obs_var + spread))
    factor = -0.5 * tempering(partial_value, count)
    padded = with_halo(state, (("lon", 0),), HALO)
    terms = factor * (obs_value[:, None] - seen) ** 2 / obs_var[:, None]
    local = jax.ops.segment_sum(terms, obs_index, num_segments=lon_dev * lat)
    misfit = with_halo(local.reshape(lon_dev, lat, members), (("lon", 0),), HALO)
    scale = 1.0
    state_pad = jnp.pad(padded, ((0, 0), (0, 0), (HALO, HALO), (0, 0)))
    mis_pad = jnp.pad(misfit, ((0, 0), (HALO, HALO), (0, 0)))[:, None]
    win = windows(state_pad)
    gram = gram_part(win, 0, span)
    result = analyse(win, windows(mis_pad), scale, gram)
    return result.reshape(lon_dev, nvar, lat, members)


def solution(mesh):
    return jax.shard_map(
        on_device,
        mesh=mesh,
        in_specs=(
            P(("ens", "lon"), None, None, None),
            P(("ens", "lon")),
            P(("ens", "lon")),
            P(("ens", "lon")),
        ),
        out_specs=P(("ens", "lon"), None, None, None),
        check_vma=False,
    )
```

profile of v0, /device:TPU:0, one launch (start us, length us, event | category | flops | bytes accessed | tf_op | source)
XLA Modules:
  0.0 96.0 jit_solution(521357441232246632)
XLA Ops:
  0.0 1.3 %fusion.64 = (bf16[4,4,64,256]{3,2,1,0:T(8,128)(2,1)S(1)}, bf16[4,4,64,256]{3,2,1,0:T(8,128)(2,1)S(1)}) fusion(bf16[8,4,64,256]{3,2,1,0:T(8,128)(2,1)} %param.4), kind=kLoop, calls=%fused_computation.137 | loop fusion | bytes 2097152 | tf_op jit(solution)/shard_map/slice | solution.py:18
  1.3 5.5 %collective-permute-start.3 = (bf16[4,4,64,256]{3,2,1,0:T(8,128)(2,1)S(1)}, bf16[4,4,64,256]{3,2,1,0:T(8,128)(2,1)S(1)}, u32[]{:S(2)}, u32[]{:S(2)}) collective-permute-start(bf16[4,4,64,256]{3,2,1,0:T(8,128)(2,1)S(1)} %get-tuple-element.14), channel_id=1, source_target_pairs={{1,0},{2,1},{3,2},{4,3},{5,4},{6,5},{7,6},{8,7},{9,8},{10,9},{11,1... | collective-permute-start | bytes 1572872 | tf_op jit(solution)/shard_map/ppermute | solution.py:23
  6.9 0.0 copy-done.7
  6.9 0.0 slice-done
  6.9 1.2 %gather_fusion = bf16[256,256]{1,0:T(8,128)(2,1)S(1)} fusion(bf16[512,256]{1,0:T(8,128)(2,1)S(1)} %bitcast.68, s32[1024]{0:T(1024)S(1)} %pad_clamp_fusion), kind=kCustom, calls=%fused_computation | custom fusion | bytes 263168 | tf_op jit(solution)/shard_map/jit(_take)/gather | solution.py:86
  8.0 0.2 convert_reduce_fusion
  8.2 0.2 fusion.41
  8.5 0.0 copy-done.5
  8.5 0.0 copy-done.6
  8.5 0.6 fusion.55
  9.1 0.0 collective-permute-start.2
  9.1 34.6 %psum.7 = f32[]{:T(128)} all-reduce(f32[]{:T(128)} %fusion.55), channel_id=1, replica_groups=mesh['ens'=2,'lon'=16] {'lon'}, use_global_device_ids=true, to_apply=%region_3.4 | all-reduce | flops 1 | bytes 8 | tf_op jit(solution)/shard_map/psum | solution.py:77
  44.4 2.2 %scatter_custom_fusion = f32[512,256]{1,0:T(8,128)S(1)} fusion(s32[256]{0:T(256)S(1)} %copy-done.7, f32[]{:T(128)} %constant.24.clone.1, f32[256]{0:T(256)S(1)} %copy-done.5, f32[256]{0:T(256)S(1)} %copy-done.6, f32[]{:T(128)S(6)} %mul_shard_map.6, bf16[256,256]{1,0:T(8,128)(2,1)S(1)} %gather_fusion, pred[256]{0:T(512)(128)(4,1)S(1)} %compare_and_fusion), kind=kCustom, calls=%fused_computation.88 | custom fusion | flops 458752 | bytes 657928 | tf_op jit(solution)/shard_map/scatter-add | solution.py:93
  46.7 0.7 fusion.65
  47.4 0.0 collective-permute-start.1
  47.4 0.5 collective-permute-start
  47.9 0.8 broadcast_multiply_fusion
  49.4 2.2 %collective-permute-done.1 = f32[4,64,256]{2,1,0:T(8,128)S(1)} collective-permute-done((f32[4,64,256]{2,1,0:T(8,128)}, f32[4,64,256]{2,1,0:T(8,128)S(1)}, u32[]{:S(2)}, u32[]{:S(2)}) %collective-permute-start.1) | collective-permute-done | bytes 262176 | tf_op jit(solution)/shard_map/ppermute | solution.py:23
  51.6 4.3 %collective-permute-done = f32[4,64,256]{2,1,0:T(8,128)S(1)} collective-permute-done((f32[4,64,256]{2,1,0:T(8,128)S(1)}, f32[4,64,256]{2,1,0:T(8,128)S(1)}, u32[]{:S(2)}, u32[]{:S(2)}) %collective-permute-start) | collective-permute-done | bytes 262176 | tf_op jit(solution)/shard_map/ppermute | solution.py:21
  56.0 0.1 select_maximum_fusion
  56.1 0.1 slice_bitcast_fusion.3
  56.2 0.0 copy-start.4
  56.2 0.1 fusion.32
  56.3 1.2 %fusion.13 = f32[1,8,256,1]{2,0,1,3:T(1,128)S(1)} fusion(f32[16,16,1,1]{1,2,3,0:T(1,128)S(1)} %bitcast.72, f32[1,8,1,9,8,256]{5,4,3,1,2,0:T(8,128)S(1)} %get-tuple-element.12, f32[1,8,1,9,8,256]{5,4,3,1,2,0:T(8,128)S(1)} %get-tuple-element.11, f32[1,16,1,8,8,256]{5,4,3,1,2,0:T(8,128)S(1)} %fusion.32), kind=kOutput, calls=%fused_computation.26 | convolution fusion | flops 7340032 | bytes 2237440 | tf_op jit(solution)/shard_map/apxbqm,pq->abm/dot_general | solution.py:59
  57.5 0.1 bitcast_reduce_fusion
  57.6 0.2 fusion.52
  57.8 0.0 collective-permute-done.3
  57.8 0.0 collective-permute-done.2
  57.9 0.0 copy-done.4
  57.9 1.4 %fusion.9 = bf16[16,4,72,256]{3,2,1,0:T(8,128)(2,1)S(1)} fusion(bf16[4,4,64,256]{3,2,1,0:T(8,128)(2,1)S(1)} %collective-permute-done.3, bf16[8,4,64,256]{3,2,1,0:T(8,128)(2,1)S(1)} %copy-done.4, bf16[4,4,64,256]{3,2,1,0:T(8,128)(2,1)S(1)} %collective-permute-done.2), kind=kLoop, calls=%fused_computation.18 | loop fusion | flops 14155776 | bytes 4456448 | tf_op jit(solution)/shard_map/concatenate | solution.py:19
  59.3 0.2 slice_bitcast_fusion.1
  59.4 0.5 fusion.10
  59.9 0.0 copy-start
  59.9 0.6 copy_bitcast_fusion
  60.5 0.9 copy-done
  61.4 0.5 copy-done.2
  61.9 2.0 %fusion.25 = f32[8,256,256]{2,1,0:T(8,128)S(1)} fusion(bf16[1,16,4,8,8,256]{5,4,3,2,1,0:T(8,128)(2,1)S(1)} %get-tuple-element.8, bf16[1,16,4,8,8,256]{5,4,3,2,1,0:T(8,128)(2,1)S(1)} %get-tuple-element.7, bf16[16,4,8,8,256]{4,3,1,0,2:T(8,128)(2,1)S(1)} %get-tuple-element.19, bf16[16,4,8,8,256]{4,3,1,0,2:T(8,128)(2,1)S(1)} %get-tuple-element.20, ...), kind=kOutput, calls=%fused_computation.59 | convolution fusion | flops 1094713344 | bytes 10486784 | tf_op jit(solution)/shard_map/apvbqm,apvbqn->abmn/dot_general | solution.py:51
  63.9 16.4 %copy.10 = f32[8,256,256]{0,2,1:T(8,128)} copy(f32[8,256,256]{2,1,0:T(8,128)S(1)} %fusion.25) | data formatting | bytes 4194304 | tf_op jit(solution)/shard_map/apvbqm,apvbqn->abmn/dot_general | solution.py:51
  80.3 2.3 %gather_fusion.1 = f32[256,8]{1,0:T(8,128)S(1)} fusion(f32[8,256,256]{0,2,1:T(8,128)} %copy.10, s32[256]{0:T(256)S(1)} %bitcast.67), kind=kCustom, calls=%fused_computation.1 | custom fusion | bytes 18432 | tf_op jit(solution)/shard_map/jit(diagonal)/gather | solution.py:57
  82.6 0.1 copy.11
  82.7 0.9 fusion.17
  83.5 0.8 exponential_reduce_fusion.7
  84.4 0.1 multiply_subtract_fusion.7
  84.4 0.4 fusion.18
  84.8 0.5 exponential_reduce_fusion.6
  85.4 0.4 fusion.19
  85.8 0.9 exponential_reduce_fusion.5
  86.7 0.1 multiply_subtract_fusion.5
  86.7 0.4 fusion.20
  87.1 0.5 exponential_reduce_fusion.4
  87.7 0.4 fusion.21
  88.1 0.9 exponential_reduce_fusion.3
  89.0 0.1 multiply_subtract_fusion.3
  89.0 0.4 fusion.22
  89.4 0.5 exponential_reduce_fusion.2
  90.0 0.4 fusion.23
  90.4 0.9 exponential_reduce_fusion.1
  91.2 0.1 multiply_subtract_fusion.1
  91.3 0.4 fusion.24
  91.7 0.5 exponential_reduce_fusion
  92.3 0.7 copy-done.1
  92.9 0.6 copy-done.3
  93.6 1.3 %fusion.30 = bf16[1,8,4,8,8,256]{5,4,2,1,3,0:T(8,128)(2,1)S(1)} fusion(f32[8,256,256]{2,1,0:T(8,128)S(1)} %get-tuple-element.6, f32[8,256]{1,0:T(8,128)S(1)} %multiply_subtract_fusion, f32[8,256]{1,0:T(8,128)S(1)} %multiply_subtract_fusion.1, bf16[1,16,4,8,8,256]{5,4,3,2,1,0:T(8,128)(2,1)S(1)} %copy-done.1, bf16[1,16,4,8,8,256]{5,4,3,2,1,0:T(8,128)(2,1)S(1)} %copy-done.3), kind=kOutput, calls=%fused_computation.61 | convolution fusion | flops 273678336 | bytes 7356416 | tf_op jit(solution)/shard_map/apvbqi,abij->apvbqj/dot_general | solution.py:72
  94.9 1.1 %copy.50 = bf16[1,8,4,8,8,256]{5,4,3,2,1,0:T(8,128)(2,1)} copy(bf16[1,8,4,8,8,256]{5,4,2,1,3,0:T(8,128)(2,1)S(1)} %fusion.30) | data formatting | bytes 2097152 | tf_op jit(solution)/shard_map/convert_element_type | solution.py:73
  (27 shorter events, 0.1 us)
Async XLA Ops:
  0.0 6.9 %slice-start = ((bf16[8,4,64,256]{3,2,1,0:T(8,128)(2,1)}), bf16[8,1,64,256]{3,2,1,0:T(8,128)(2,1)S(1)}, s32[]{:S(2)}) async-start(bf16[8,4,64,256]{3,2,1,0:T(8,128)(2,1)} %param.4), calls=%async_computation | async-start | bytes 524288 | tf_op jit(solution)/shard_map/slice | solution.py:85
  0.0 6.9 %copy-start.7 = (s32[256]{0:T(256)S(1)}, s32[256]{0:T(256)}, u32[]{:S(2)}) copy-start(s32[256]{0:T(256)} %param.5) | copy-start | bytes 3076
  0.0 8.5 %copy-start.5 = (f32[256]{0:T(256)S(1)}, f32[256]{0:T(256)}, u32[]{:S(2)}) copy-start(f32[256]{0:T(256)} %param.7) | copy-start | bytes 3076
  0.0 8.5 %copy-start.6 = (f32[256]{0:T(256)S(1)}, f32[256]{0:T(256)}, u32[]{:S(2)}) copy-start(f32[256]{0:T(256)} %param.6) | copy-start | bytes 3076
  1.3 56.5 %collective-permute-start.3 = (bf16[4,4,64,256]{3,2,1,0:T(8,128)(2,1)S(1)}, bf16[4,4,64,256]{3,2,1,0:T(8,128)(2,1)S(1)}, u32[]{:S(2)}, u32[]{:S(2)}) collective-permute-start(bf16[4,4,64,256]{3,2,1,0:T(8,128)(2,1)S(1)} %get-tuple-element.14), channel_id=1, source_target_pairs={{1,0},{2,1},{3,2},{4,3},{5,4},{6,5},{7,6},{8,7},{9,8},{10,9},{11,1... | collective-permute-start | bytes 1572872 | tf_op jit(solution)/shard_map/ppermute | solution.py:23
  9.1 48.7 %collective-permute-start.2 = (bf16[4,4,64,256]{3,2,1,0:T(8,128)(2,1)S(1)}, bf16[4,4,64,256]{3,2,1,0:T(8,128)(2,1)S(1)}, u32[]{:S(2)}, u32[]{:S(2)}) collective-permute-start(bf16[4,4,64,256]{3,2,1,0:T(8,128)(2,1)S(1)} %get-tuple-element.13), channel_id=1, source_target_pairs={{0,1},{1,2},{2,3},{3,4},{4,5},{5,6},{6,7},{7,8},{8,9},{9,10},{10,1... | collective-permute-start | bytes 1572872 | tf_op jit(solution)/shard_map/ppermute | solution.py:21
  47.4 4.2 %collective-permute-start.1 = (f32[4,64,256]{2,1,0:T(8,128)}, f32[4,64,256]{2,1,0:T(8,128)S(1)}, u32[]{:S(2)}, u32[]{:S(2)}) collective-permute-start(f32[4,64,256]{2,1,0:T(8,128)} %bitcast.3), channel_id=1, source_target_pairs={{1,0},{2,1},{3,2},{4,3},{5,4},{6,5},{7,6},{8,7},{9,8},{10,9},{11,1... | collective-permute-start | bytes 786440 | tf_op jit(solution)/shard_map/ppermute | solution.py:23
  47.4 8.5 %collective-permute-start = (f32[4,64,256]{2,1,0:T(8,128)S(1)}, f32[4,64,256]{2,1,0:T(8,128)S(1)}, u32[]{:S(2)}, u32[]{:S(2)}) collective-permute-start(f32[4,64,256]{2,1,0:T(8,128)S(1)} %bitcast.70), channel_id=1, source_target_pairs={{0,1},{1,2},{2,3},{3,4},{4,5},{5,6},{6,7},{7,8},{8,9},{9,10},{10,1... | collective-permute-start | bytes 786440 | tf_op jit(solution)/shard_map/ppermute | solution.py:21
  56.2 1.7 %copy-start.4 = (bf16[8,4,64,256]{3,2,1,0:T(8,128)(2,1)S(1)}, bf16[8,4,64,256]{3,2,1,0:T(8,128)(2,1)}, u32[]{:S(2)}) copy-start(bf16[8,4,64,256]{3,2,1,0:T(8,128)(2,1)} %param.4) | copy-start | bytes 3145732
  59.9 1.5 %copy-start = (bf16[1,16,4,8,8,256]{5,4,3,2,1,0:T(8,128)(2,1)}, bf16[1,16,4,8,8,256]{5,4,3,2,1,0:T(8,128)(2,1)S(1)}, u32[]{:S(2)}) copy-start(bf16[1,16,4,8,8,256]{5,4,3,2,1,0:T(8,128)(2,1)S(1)} %get-tuple-element.7) | copy-start | bytes 6291460
  59.9 2.0 %copy-start.2 = (bf16[1,16,4,8,8,256]{5,4,3,2,1,0:T(8,128)(2,1)}, bf16[1,16,4,8,8,256]{5,4,3,2,1,0:T(8,128)(2,1)S(1)}, u32[]{:S(2)}) copy-start(bf16[1,16,4,8,8,256]{5,4,3,2,1,0:T(8,128)(2,1)S(1)} %get-tuple-element.8) | copy-start | bytes 6291460
  91.3 1.6 %copy-start.1 = (bf16[1,16,4,8,8,256]{5,4,3,2,1,0:T(8,128)(2,1)S(1)}, bf16[1,16,4,8,8,256]{5,4,3,2,1,0:T(8,128)(2,1)}, u32[]{:S(2)}) copy-start(bf16[1,16,4,8,8,256]{5,4,3,2,1,0:T(8,128)(2,1)} %copy-done) | copy-start | bytes 6291460
  91.3 2.2 %copy-start.3 = (bf16[1,16,4,8,8,256]{5,4,3,2,1,0:T(8,128)(2,1)S(1)}, bf16[1,16,4,8,8,256]{5,4,3,2,1,0:T(8,128)(2,1)}, u32[]{:S(2)}) copy-start(bf16[1,16,4,8,8,256]{5,4,3,2,1,0:T(8,128)(2,1)} %copy-done.2) | copy-start | bytes 6291460
where the time goes:
time: 96.2 us; the launch traced here: 96 us
  blocking collectives  34.6 us (36%)
  local copies, waits for them, and re-layouts  26.6 us (28%)
  other arithmetic  15.9 us (17%)
  waiting for transfers between devices  6.56 us (7%)
  starting transfers between devices  6.04 us (6%)
  matrix products  4.47 us (5%)
  between operations  1.75 us (2%)
    psum x1, blocking collectives, tempering(): return count / lax.psum(partial_value, 'lon')  34.6 us
    dot_general x1, local copies, waits for them, and re-layouts, gram_part(): jnp.einsum('apvbqm,apvbqn->abmn', weighted, win, preferred_element_type=j...  16.4 us
    ppermute x2, starting transfers between devices, with_halo(): lax.ppermute(head, axis, [((i + 1) % count, i) for i in range(count)])  5.53 us
    ppermute x2, waiting for transfers between devices, with_halo(): lax.ppermute(tail, axis, [(i, (i + 1) % count) for i in range(count)])  4.33 us
    reduce_sum x4, other arithmetic, analyse(): jax.nn.logsumexp((pot_g[..., None, :] - cost) / EPS, axis=-1)  3.45 us
    unnamed x16, local copies, waits for them, and re-layouts  2.76 us
    gather x2, local copies, waits for them, and re-layouts, analyse(): diag = jnp.diagonal(gram, axis1=2, axis2=3)  2.38 us
    scatter-add x1, other arithmetic, on_device(): local = jax.ops.segment_sum(terms, obs_index, num_segments=lon_dev * lat)  2.24 us
  transfers between devices with their start and end apart: 4, of which 2 were waited for; matrix products, arithmetic and copies ran while one was open for 8% of the time, Pallas kernels for 0%

commit v1 on v0

v1 whole, which is shorter than its diff:
```python
import functools
import jax
import jax.numpy as jnp
from jax import lax
from jax.experimental import pallas as pl
from jax.experimental.pallas import tpu as pltpu
from jax.sharding import PartitionSpec as P

REGION = 8
HALO = 4
SWEEPS = 4
EPS = 0.05
TILE = 16
MESH = pl.DeviceIdType.MESH


def line(place):
    dist = jnp.maximum(0.0, jnp.maximum(HALO - place, place - (HALO + REGION - 1)))
    return jnp.maximum(0.0, 1.0 - dist / (HALO + 1))


def rho_sum():
    return sum(
        1.0 - max(0, HALO - p, p - (HALO + REGION - 1)) / (HALO + 1) for p in range(REGION + 2 * HALO)
    ) ** 2


def row_lse(pot_g, cost_ref):
    members = cost_ref.shape[0]
    parts = []
    for start in range(0, members, 64):
        arg = pot_g - cost_ref[start : start + 64, :]
        top = jnp.max(arg, axis=1, keepdims=True)
        parts.append(top + jnp.log(jnp.sum(jnp.exp(arg - top), axis=1, keepdims=True)))
    return jnp.concatenate(parts, axis=0)


def column_lse(pot_f, cost_ref):
    arg = pot_f - cost_ref[...]
    top = jnp.max(arg, axis=0, keepdims=True)
    return top + jnp.log(jnp.sum(jnp.exp(arg - top), axis=0, keepdims=True))


def kernel(
    count, state_ref, index_ref, value_ref, var_ref, out_ref,
    buf, win, wgt, own, cost, logw, parts, like_out, like_in, out_buf,
    own_sem, halo_send, halo_recv, like_send, like_recv, part_send, part_recv, out_sem,
):
    lon_dev, nvar, lat, members = state_ref.shape
    span = REGION + 2 * HALO
    chunks = lat // TILE
    regions = lat // REGION
    me = lax.axis_index("lon")
    right, left = lax.rem(me + 1, count), lax.rem(me + count - 1, count)

    barrier = pltpu.get_barrier_semaphore()

    @pl.loop(1, count)
    def _(hop):
        pl.semaphore_signal(
            barrier, inc=1, device_id={"lon": lax.rem(me + hop, count)}, device_id_type=MESH
        )

    own_copy = pltpu.make_async_copy(
        state_ref, buf.at[pl.ds(HALO, lon_dev), :, pl.ds(TILE, lat), :], own_sem
    )
    own_copy.start()
    blank = jnp.zeros((span, nvar, TILE, members), jnp.bfloat16)
    buf[:, :, 0:TILE, :] = blank
    buf[:, :, TILE + lat : 2 * TILE + lat, :] = blank
    pl.semaphore_wait(barrier, count - 1)

    def halo_copy(side, chunk):
        return pltpu.make_async_remote_copy(
            src_ref=state_ref.at[
                pl.ds(lon_dev - HALO if side == 0 else 0, HALO), :, pl.ds(chunk * TILE, TILE), :
            ],
            dst_ref=buf.at[
                pl.ds(0 if side == 0 else HALO + lon_dev, HALO), :, pl.ds(TILE + chunk * TILE, TILE), :
            ],
            send_sem=halo_send.at[side, chunk],
            recv_sem=halo_recv.at[side, chunk],
            device_id={"lon": right if side == 0 else left},
            device_id_type=MESH,
        )

    for chunk in range(min(2, chunks)):
        for side in range(2):
            halo_copy(side, chunk).start()
    own_copy.wait()

    index = index_ref[...]
    value = value_ref[...]
    var = var_ref[...]
    nobs = index.shape[1]
    rows = buf[HALO : HALO + lon_dev, 0, TILE : TILE + lat, :].reshape(lon_dev * lat, members)
    onehot = (lax.broadcasted_iota(jnp.int32, (lon_dev * lat, nobs), 0) == index).astype(jnp.float32)
    seen = lax.dot_general(
        rows, onehot.astype(jnp.bfloat16), (((0,), (0,)), ((), ())), preferred_element_type=jnp.float32
    )
    centre = jnp.sum(seen, axis=0, keepdims=True) / members
    spread = jnp.sum((seen - centre) ** 2, axis=0, keepdims=True) / (members - 1)
    partial_value = jnp.sum((value - centre) ** 2 / (var + spread), axis=1, keepdims=True)
    parts[0] = jnp.broadcast_to(partial_value, (8, 128))

    lon_of = jnp.zeros(index.shape, jnp.int32)
    for lon in range(1, lon_dev):
        lon_of = lon_of + (index >= lon * lat).astype(jnp.int32)
    lat_of = (index - lon_of * lat).astype(jnp.float32)
    lon_of = lon_of.astype(jnp.float32)
    region = lax.broadcasted_iota(jnp.int32, (regions, nobs), 0).astype(jnp.float32)
    weight = line(lat_of - region * REGION + HALO) / var
    weights = jnp.concatenate(
        [
            weight,
            weight * line(lon_of - lon_dev + HALO),
            weight * line(lon_of + lon_dev + HALO),
        ],
        axis=0,
    )
    square = (value - seen) ** 2
    like = lax.dot_general(
        weights, square, (((1,), (1,)), ((), ())),
        precision=lax.Precision.HIGHEST, preferred_element_type=jnp.float32,
    )
    like_out[0] = like[regions : 2 * regions]
    like_out[1] = like[2 * regions : 3 * regions]
    like_own = like[0:regions]

    def part_copy(hop):
        return pltpu.make_async_remote_copy(
            src_ref=parts.at[0],
            dst_ref=parts.at[hop],
            send_sem=part_send.at[hop],
            recv_sem=part_recv.at[hop],
            device_id={"lon": lax.rem(me + hop, count)},
            device_id_type=MESH,
        )

    def like_copy(side):
        return pltpu.make_async_remote_copy(
            src_ref=like_out.at[side],
            dst_ref=like_in.at[side],
            send_sem=like_send.at[side],
            recv_sem=like_recv.at[side],
            device_id={"lon": right if side == 0 else left},
            device_id_type=MESH,
        )

    @pl.loop(1, count)
    def _(hop):
        part_copy(hop).start()

    for side in range(2):
        like_copy(side).start()
    for chunk in range(2, chunks):
        for side in range(2):
            halo_copy(side, chunk).start()

    def pair_build(step, lons):
        base = pl.multiple_of(step * TILE, TILE)
        place = lax.broadcasted_iota(jnp.int32, (span, members), 0).astype(jnp.float32)
        taper = line(place)
        for lon in lons:
            rho = taper * (1.0 - max(0, HALO - lon, lon - (HALO + REGION - 1)) / (HALO + 1))
            for variable in range(nvar):
                x = buf[lon, variable, pl.ds(base, 3 * TILE), :].astype(jnp.float32)
                y = x[TILE - HALO : TILE + 2 * REGION + HALO]
                for a in range(2):
                    w = y[a * REGION : a * REGION + span]
                    win[a, lon, variable] = w.astype(jnp.bfloat16)
                    wgt[a, lon, variable] = (w * rho).astype(jnp.bfloat16)
                    if HALO <= lon < HALO + REGION:
                        own[a, lon - HALO, variable] = x[
                            TILE + a * REGION : TILE + (a + 1) * REGION
                        ]

    scale = 1.0 / (nvar * rho_sum() * EPS)

    def gram_cost(a):
        depth = span * nvar * span
        gram = lax.dot_general(
            wgt[a].reshape(depth, members), win[a].reshape(depth, members),
            (((0,), (0,)), ((), ())), preferred_element_type=jnp.float32,
        )
        shape = (members, members)
        eye = lax.broadcasted_iota(jnp.int32, shape, 0) == lax.broadcasted_iota(jnp.int32, shape, 1)
        only = jnp.where(eye, gram, 0.0)
        diag_row = jnp.sum(only, axis=0, keepdims=True)
        diag_col = jnp.sum(only, axis=1, keepdims=True)
        cost[a] = (diag_col + diag_row - 2.0 * gram) * scale

    def body(step, carry):
        pair_build(step, range(HALO, HALO + lon_dev))
        for chunk in range(chunks):
            @pl.when(step == max(chunk - 1, 0))
            def _():
                for side in range(2):
                    halo_copy(side, chunk).wait_recv()

        pair_build(step, list(range(HALO)) + list(range(HALO + lon_dev, span)))
        for a in range(2):
            gram_cost(a)

        @pl.when(step == 0)
        def _():
            @pl.loop(1, count)
            def _(hop):
                part_copy(hop).wait_recv()

            total = lax.fori_loop(
                1, count, lambda hop, acc: acc + parts[hop], parts[0]
            )[0:1, 0:1]
            factor = -0.5 * (count * nobs) / total
            for side in range(2):
                like_copy(side).wait_recv()
            every = factor * (like_own_ref(like_in) + like_in[0] + like_in[1])
            top = jnp.max(every, axis=1, keepdims=True)
            every = every - (top + jnp.log(jnp.sum(jnp.exp(every - top), axis=1, keepdims=True)))
            turned = jnp.transpose(every)
            for r in range(regions):
                logw[r] = jnp.broadcast_to(turned[:, r : r + 1], (members, 128))

        pot_f = [None, None]
        pot_g = [jnp.zeros((1, members), jnp.float32)] * 2
        for sweep in range(SWEEPS):
            for a in range(2):
                pot_f[a] = logw[2 * step + a][:, 0:1] - row_lse(pot_g[a], cost.at[a])
            for a in range(2):
                pot_g[a] = -jnp.log(jnp.float32(members)) - column_lse(pot_f[a], cost.at[a])
        results = []
        for a in range(2):
            transport = (members * jnp.exp(pot_f[a] + pot_g[a] - cost[a])).astype(jnp.bfloat16)
            lhs = own[a].reshape(lon_dev * nvar * REGION, members).astype(jnp.bfloat16)
            res = jnp.dot(lhs, transport, preferred_element_type=jnp.float32)
            results.append(res.reshape(lon_dev, nvar, REGION, members))
        out_buf[step] = jnp.concatenate(results, axis=2).astype(jnp.bfloat16)
        out_copy(step).start()
        return carry

    def like_own_ref(_):
        return like_in[2]

    def out_copy(step):
        return pltpu.make_async_copy(
            out_buf.at[step],
            out_ref.at[:, :, pl.ds(pl.multiple_of(step * TILE, TILE), TILE), :],
            out_sem.at[step],
        )

    like_in[2] = like_own
    lax.fori_loop(0, chunks, body, 0)

    for chunk in range(chunks):
        for side in range(2):
            halo_copy(side, chunk).wait_send()
    for side in range(2):
        like_copy(side).wait_send()

    @pl.loop(1, count)
    def _(hop):
        part_copy(hop).wait_send()

    @pl.loop(0, chunks)
    def _(step):
        out_copy(step).wait()


def on_device(state, obs_index, obs_value, obs_var):
    lon_dev, nvar, lat, members = state.shape
    nobs = obs_index.shape[0]
    count = lax.axis_size("lon")
    span = REGION + 2 * HALO
    chunks = lat // TILE
    regions = lat // REGION
    dma = pltpu.SemaphoreType.DMA
    vmem = pl.BlockSpec(memory_space=pltpu.VMEM)
    hbm = pl.BlockSpec(memory_space=pl.ANY)
    return pl.pallas_call(
        functools.partial(kernel, count),
        out_shape=jax.ShapeDtypeStruct(state.shape, state.dtype),
        in_specs=[hbm, vmem, vmem, vmem],
        out_specs=hbm,
        scratch_shapes=[
            pltpu.VMEM((span, nvar, lat + 2 * TILE, members), jnp.bfloat16),
            pltpu.VMEM((2, span, nvar, span, members), jnp.bfloat16),
            pltpu.VMEM((2, span, nvar, span, members), jnp.bfloat16),
            pltpu.VMEM((2, lon_dev, nvar, REGION, members), jnp.float32),
            pltpu.VMEM((2, members, members), jnp.float32),
            pltpu.VMEM((regions, members, 128), jnp.float32),
            pltpu.VMEM((count, 8, 128), jnp.float32),
            pltpu.VMEM((2, regions, members), jnp.float32),
            pltpu.VMEM((3, regions, members), jnp.float32),
            pltpu.VMEM((chunks, lon_dev, nvar, TILE, members), jnp.bfloat16),
            dma, dma((2, chunks)), dma((2, chunks)), dma((2,)), dma((2,)),
            dma((count,)), dma((count,)), dma((chunks,)),
        ],
        compiler_params=pltpu.CompilerParams(
            collective_id=0, has_side_effects=True, vmem_limit_bytes=48 << 20
        ),
        name="analysis",
    )(
        state,
        obs_index.reshape(1, nobs),
        obs_value.reshape(1, nobs),
        obs_var.reshape(1, nobs),
    )


def solution(mesh):
    return jax.shard_map(
        on_device,
        mesh=mesh,
        in_specs=(
            P(("ens", "lon"), None, None, None),
            P(("ens", "lon")),
            P(("ens", "lon")),
            P(("ens", "lon")),
        ),
        out_specs=P(("ens", "lon"), None, None, None),
        check_vma=False,
    )
```

time: 96.2 us -> 32.8 us (0.34)
  blocking collectives: 34.6 us -> 0 us
  Pallas kernels: 0 us -> 29.7 us
  local copies, waits for them, and re-layouts: 26.6 us -> 2.9 us
  other arithmetic: 15.9 us -> 0 us
  waiting for transfers between devices: 6.56 us -> 0 us
  starting transfers between devices: 6.04 us -> 0 us
  matrix products: 4.47 us -> 0 us
  between operations: 1.75 us -> 0.01 us
    psum x1 -> x0, blocking collectives: 34.6 us -> none  [tempering(): return count / lax.psum(partial_value, 'lon')]
    pallas_call x0 -> x1, Pallas kernels: none -> 29.7 us  [on_device(): pl.pallas_call(functools.partial(kernel, count), out_shape=jax.ShapeDtype...]
    dot_general x1 -> x0, local copies, waits for them, and re-layouts: 16.4 us -> none  [gram_part(): jnp.einsum('apvbqm,apvbqn->abmn', weighted, win, preferred_element_type=j...]
    reduce_sum x12 -> x0, other arithmetic: 6.74 us -> none  [the longest x4 3.45 us: analyse(): jax.nn.logsumexp((pot_g[..., None, :] - cost) / EPS, axis=-1)]
    ppermute x4 -> x0, waiting for transfers between devices: 6.56 us -> none  [the longest x2 4.33 us: with_halo(): lax.ppermute(tail, axis, [(i, (i + 1) % count) for i in range(count)])]
    ppermute x4 -> x0, starting transfers between devices: 6.04 us -> none  [the longest x2 5.53 us: with_halo(): lax.ppermute(head, axis, [((i + 1) % count, i) for i in range(count)])]
    dot_general x3 -> x0, matrix products: 4.47 us -> none  [the longest x1 1.96 us: gram_part(): jnp.einsum('apvbqm,apvbqn->abmn', weighted, win, preferred_element_type=j...]
    reduce_max x9 -> x0, other arithmetic: 3.63 us -> none  [the longest x4 2.07 us: analyse(): jax.nn.logsumexp((pot_g[..., None, :] - cost) / EPS, axis=-1)]
  transfers between devices with their start and end apart: 4 -> 0, of which waited for: 2 -> 0; matrix products, arithmetic and copies ran while one was open for 8% -> 0% of each run, Pallas kernels for 0% -> 0%
where the time goes in v1:
time: 32.8 us; the launch traced here: 32.6 us
  Pallas kernels  29.7 us (91%)
  local copies, waits for them, and re-layouts  2.9 us (9%)
    pallas_call x1, Pallas kernels, on_device(): pl.pallas_call(functools.partial(kernel, count), out_shape=jax.ShapeDtype...  29.7 us
    unnamed x9, local copies, waits for them, and re-layouts  2.9 us

profile of v1, /device:TPU:0, one launch (start us, length us, event | category | flops | bytes accessed | tf_op | source)
XLA Modules:
  0.0 32.6 jit_solution(15113838938249861704)
XLA Ops:
  0.0 0.0 copy-start.2
  0.0 0.0 copy-start.3
  0.0 0.0 copy-start.1
  0.0 0.7 %copy-done.2 = f32[256]{0:T(256)S(1)} copy-done((f32[256]{0:T(256)S(1)}, f32[256]{0:T(256)}, u32[]{:S(2)}) %copy-start.2) | copy-done | bytes 1048
  0.7 0.0 copy-done.3
  0.7 0.0 copy-done.1
  0.7 0.0 copy-start
  0.7 1.2 %copy-done = bf16[8,4,64,256]{3,2,1,0:T(8,128)(2,1)S(1)} copy-done((bf16[8,4,64,256]{3,2,1,0:T(8,128)(2,1)S(1)}, bf16[8,4,64,256]{3,2,1,0:T(8,128)(2,1)}, u32[]{:S(2)}) %copy-start) | copy-done | bytes 1048600
  1.9 29.7 %analysis.1 = bf16[8,4,64,256]{3,2,1,0:T(8,128)(2,1)S(1)} custom-call(bf16[8,4,64,256]{3,2,1,0:T(8,128)(2,1)S(1)} %copy-done, s32[1,256]{1,0:T(1,128)S(1)} %bitcast.3, f32[1,256]{1,0:T(1,128)S(1)} %bitcast.4, f32[1,256]{1,0:T(1,128)S(1)} %bitcast.5), custom_call_target="tpu_custom_call" | custom-call | tf_op jit(solution)/shard_map/analysis/pallas_call | solution.py:279
  31.6 1.0 %copy.6 = bf16[8,4,64,256]{3,2,1,0:T(8,128)(2,1)} copy(bf16[8,4,64,256]{3,2,1,0:T(8,128)(2,1)S(1)} %analysis.1) | data formatting | bytes 2097152
Async XLA Ops:
  0.0 0.7 %copy-start.2 = (f32[256]{0:T(256)S(1)}, f32[256]{0:T(256)}, u32[]{:S(2)}) copy-start(f32[256]{0:T(256)} %param.6) | copy-start | bytes 3076
  0.0 0.7 %copy-start.3 = (f32[256]{0:T(256)S(1)}, f32[256]{0:T(256)}, u32[]{:S(2)}) copy-start(f32[256]{0:T(256)} %param.7) | copy-start | bytes 3076
  0.0 0.7 %copy-start.1 = (s32[256]{0:T(256)S(1)}, s32[256]{0:T(256)}, u32[]{:S(2)}) copy-start(s32[256]{0:T(256)} %param.5) | copy-start | bytes 3076
  0.7 1.2 %copy-start = (bf16[8,4,64,256]{3,2,1,0:T(8,128)(2,1)S(1)}, bf16[8,4,64,256]{3,2,1,0:T(8,128)(2,1)}, u32[]{:S(2)}) copy-start(bf16[8,4,64,256]{3,2,1,0:T(8,128)(2,1)} %state_ref.1) | copy-start | bytes 3145732

commit v2 on v1

--- a/solution.py
+++ b/solution.py
@@ -1,4 +1,5 @@
 import functools
+import math
 import jax
 import jax.numpy as jnp
 from jax import lax
@@ -11,6 +12,8 @@
 SWEEPS = 4
 EPS = 0.05
 TILE = 16
+LANES = 128
+STRIP = 64
 MESH = pl.DeviceIdType.MESH
 
 
@@ -25,26 +28,40 @@
     ) ** 2
 
 
+def log2(x):
+    return jnp.log(x) * (1.0 / math.log(2.0))
+
+
 def row_lse(pot_g, cost_ref):
     members = cost_ref.shape[0]
     parts = []
-    for start in range(0, members, 64):
-        arg = pot_g - cost_ref[start : start + 64, :]
-        top = jnp.max(arg, axis=1, keepdims=True)
-        parts.append(top + jnp.log(jnp.sum(jnp.exp(arg - top), axis=1, keepdims=True)))
+    for start in range(0, members, STRIP):
+        args = [
+            pot_g[:, at : at + LANES] - cost_ref[start : start + STRIP, at : at + LANES]
+            for at in range(0, members, LANES)
+        ]
+        top = jnp.max(functools.reduce(jnp.maximum, args), axis=1, keepdims=True)
+        top = jnp.broadcast_to(top, (STRIP, LANES))
+        total = functools.reduce(jnp.add, [jnp.exp2(arg - top) for arg in args])
+        total = jnp.broadcast_to(jnp.sum(total, axis=1, keepdims=True), (STRIP, LANES))
+        parts.append(top + log2(total))
     return jnp.concatenate(parts, axis=0)
 
 
 def column_lse(pot_f, cost_ref):
-    arg = pot_f - cost_ref[...]
-    top = jnp.max(arg, axis=0, keepdims=True)
-    return top + jnp.log(jnp.sum(jnp.exp(arg - top), axis=0, keepdims=True))
+    members = cost_ref.shape[0]
+    parts = []
+    for at in range(0, members, LANES):
+        arg = pot_f - cost_ref[:, at : at + LANES]
+        top = jnp.max(arg, axis=0, keepdims=True)
+        parts.append(top + log2(jnp.sum(jnp.exp2(arg - top), axis=0, keepdims=True)))
+    return jnp.concatenate(parts, axis=1)
 
 
 def kernel(
-    count, state_ref, index_ref, value_ref, var_ref, out_ref,
-    buf, win, wgt, own, cost, logw, parts, like_out, like_in, out_buf,
-    own_sem, halo_send, halo_recv, like_send, like_recv, part_send, part_recv, out_sem,
+    count, state_ref, index_hbm, value_hbm, var_hbm, out_ref,
+    index_ref, value_ref, var_ref,    buf, win, wgt, own, cost, logw, parts, like_out, like_in, out_buf,
+    own_sem, obs_sem, halo_send, halo_recv, like_send, like_recv, part_send, part_recv, out_sem,
 ):
     lon_dev, nvar, lat, members = state_ref.shape
     span = REGION + 2 * HALO
@@ -65,10 +82,17 @@
         state_ref, buf.at[pl.ds(HALO, lon_dev), :, pl.ds(TILE, lat), :], own_sem
     )
     own_copy.start()
+    obs_copies = [
+        pltpu.make_async_copy(src, dst, obs_sem.at[at])
+        for at, (src, dst) in enumerate(
+            ((index_hbm, index_ref), (value_hbm, value_ref), (var_hbm, var_ref))
+        )
+    ]
+    for copy in obs_copies:
+        copy.start()
     blank = jnp.zeros((span, nvar, TILE, members), jnp.bfloat16)
     buf[:, :, 0:TILE, :] = blank
     buf[:, :, TILE + lat : 2 * TILE + lat, :] = blank
-    pl.semaphore_wait(barrier, count - 1)
 
     def halo_copy(side, chunk):
         return pltpu.make_async_remote_copy(
@@ -84,10 +108,9 @@
             device_id_type=MESH,
         )
 
-    for chunk in range(min(2, chunks)):
-        for side in range(2):
-            halo_copy(side, chunk).start()
     own_copy.wait()
+    for copy in obs_copies:
+        copy.wait()
 
     index = index_ref[...]
     value = value_ref[...]
@@ -102,6 +125,26 @@
     spread = jnp.sum((seen - centre) ** 2, axis=0, keepdims=True) / (members - 1)
     partial_value = jnp.sum((value - centre) ** 2 / (var + spread), axis=1, keepdims=True)
     parts[0] = jnp.broadcast_to(partial_value, (8, 128))
+
+    def part_copy(hop):
+        return pltpu.make_async_remote_copy(
+            src_ref=parts.at[0],
+            dst_ref=parts.at[hop],
+            send_sem=part_send.at[hop],
+            recv_sem=part_recv.at[hop],
+            device_id={"lon": lax.rem(me + hop, count)},
+            device_id_type=MESH,
+        )
+
+    pl.semaphore_wait(barrier, count - 1)
+
+    @pl.loop(1, count)
+    def _(hop):
+        part_copy(hop).start()
+
+    for chunk in range(min(2, chunks)):
+        for side in range(2):
+            halo_copy(side, chunk).start()
 
     lon_of = jnp.zeros(index.shape, jnp.int32)
     for lon in range(1, lon_dev):
@@ -127,16 +170,6 @@
     like_out[1] = like[2 * regions : 3 * regions]
     like_own = like[0:regions]
 
-    def part_copy(hop):
-        return pltpu.make_async_remote_copy(
-            src_ref=parts.at[0],
-            dst_ref=parts.at[hop],
-            send_sem=part_send.at[hop],
-            recv_sem=part_recv.at[hop],
-            device_id={"lon": lax.rem(me + hop, count)},
-            device_id_type=MESH,
-        )
-
     def like_copy(side):
         return pltpu.make_async_remote_copy(
             src_ref=like_out.at[side],
@@ -146,10 +179,6 @@
             device_id={"lon": right if side == 0 else left},
             device_id_type=MESH,
         )
-
-    @pl.loop(1, count)
-    def _(hop):
-        part_copy(hop).start()
 
     for side in range(2):
         like_copy(side).start()
@@ -175,7 +204,7 @@
                             TILE + a * REGION : TILE + (a + 1) * REGION
                         ]
 
-    scale = 1.0 / (nvar * rho_sum() * EPS)
+    scale = 1.0 / (nvar * rho_sum() * EPS * math.log(2.0))
 
     def gram_cost(a):
         depth = span * nvar * span
@@ -201,6 +230,7 @@
         pair_build(step, list(range(HALO)) + list(range(HALO + lon_dev, span)))
         for a in range(2):
             gram_cost(a)
+        first = [row_lse(jnp.zeros((1, members), jnp.float32), cost.at[a]) for a in range(2)]
 
         @pl.when(step == 0)
         def _():
@@ -211,26 +241,34 @@
             total = lax.fori_loop(
                 1, count, lambda hop, acc: acc + parts[hop], parts[0]
             )[0:1, 0:1]
-            factor = -0.5 * (count * nobs) / total
+            factor = (-0.5 * count * nobs / math.log(2.0)) / total
             for side in range(2):
                 like_copy(side).wait_recv()
             every = factor * (like_own_ref(like_in) + like_in[0] + like_in[1])
             top = jnp.max(every, axis=1, keepdims=True)
-            every = every - (top + jnp.log(jnp.sum(jnp.exp(every - top), axis=1, keepdims=True)))
+            every = every - (top + log2(jnp.sum(jnp.exp2(every - top), axis=1, keepdims=True)))
             turned = jnp.transpose(every)
             for r in range(regions):
                 logw[r] = jnp.broadcast_to(turned[:, r : r + 1], (members, 128))
 
-        pot_f = [None, None]
-        pot_g = [jnp.zeros((1, members), jnp.float32)] * 2
+        pot_f = [logw[2 * step + a] - first[a] for a in range(2)]
+        pot_g = [None, None]
         for sweep in range(SWEEPS):
             for a in range(2):
-                pot_f[a] = logw[2 * step + a][:, 0:1] - row_lse(pot_g[a], cost.at[a])
+                if sweep > 0:
+                    pot_f[a] = logw[2 * step + a] - row_lse(pot_g[a], cost.at[a])
             for a in range(2):
-                pot_g[a] = -jnp.log(jnp.float32(members)) - column_lse(pot_f[a], cost.at[a])
+                pot_g[a] = -math.log2(members) - column_lse(pot_f[a], cost.at[a])
         results = []
         for a in range(2):
-            transport = (members * jnp.exp(pot_f[a] + pot_g[a] - cost[a])).astype(jnp.bfloat16)
+            shifted = pot_g[a] + math.log2(members)
+            transport = jnp.concatenate(
+                [
+                    jnp.exp2(pot_f[a] + shifted[:, at : at + LANES] - cost[a, :, at : at + LANES])
+                    for at in range(0, members, LANES)
+                ],
+                axis=1,
+            ).astype(jnp.bfloat16)
             lhs = own[a].reshape(lon_dev * nvar * REGION, members).astype(jnp.bfloat16)
             res = jnp.dot(lhs, transport, preferred_element_type=jnp.float32)
             results.append(res.reshape(lon_dev, nvar, REGION, members))
@@ -274,14 +312,17 @@
     chunks = lat // TILE
     regions = lat // REGION
     dma = pltpu.SemaphoreType.DMA
-    vmem = pl.BlockSpec(memory_space=pltpu.VMEM)
     hbm = pl.BlockSpec(memory_space=pl.ANY)
+    pinned = pl.BlockSpec(memory_space=pltpu.HBM)
     return pl.pallas_call(
         functools.partial(kernel, count),
         out_shape=jax.ShapeDtypeStruct(state.shape, state.dtype),
-        in_specs=[hbm, vmem, vmem, vmem],
+        in_specs=[pinned] * 4,
         out_specs=hbm,
         scratch_shapes=[
+            pltpu.VMEM((1, nobs), jnp.int32),
+            pltpu.VMEM((1, nobs), jnp.float32),
+            pltpu.VMEM((1, nobs), jnp.float32),
             pltpu.VMEM((span, nvar, lat + 2 * TILE, members), jnp.bfloat16),
             pltpu.VMEM((2, span, nvar, span, members), jnp.bfloat16),
             pltpu.VMEM((2, span, nvar, span, members), jnp.bfloat16),
@@ -292,7 +333,7 @@
             pltpu.VMEM((2, regions, members), jnp.float32),
             pltpu.VMEM((3, regions, members), jnp.float32),
             pltpu.VMEM((chunks, lon_dev, nvar, TILE, members), jnp.bfloat16),
-            dma, dma((2, chunks)), dma((2, chunks)), dma((2,)), dma((2,)),
+            dma, dma((3,)), dma((2, chunks)), dma((2, chunks)), dma((2,)), dma((2,)),
             dma((count,)), dma((count,)), dma((chunks,)),
         ],
         compiler_params=pltpu.CompilerParams(
@@ -300,10 +341,7 @@
         ),
         name="analysis",
     )(
-        state,
-        obs_index.reshape(1, nobs),
-        obs_value.reshape(1, nobs),
-        obs_var.reshape(1, nobs),
+        *[pltpu.with_memory_space_constraint(x, pltpu.HBM) for x in (state, obs_index.reshape(1, nobs), obs_value.reshape(1, nobs), obs_var.reshape(1, nobs))],
     )
 
 

time: 32.8 us -> 29.5 us (0.90)
  the two profiles are of different devices: /device:TPU:0 before, /device:TPU:1 now
where the time goes in v2:
time: 29.5 us; the launch traced here: 29.3 us
  Pallas kernels  28.3 us (96%)
  local copies, waits for them, and re-layouts  0.97 us (3%)
    pallas_call x1, Pallas kernels, on_device(): pl.pallas_call(functools.partial(kernel, count), out_shape=jax.ShapeDtype...  28.3 us
    unnamed x1, local copies, waits for them, and re-layouts  0.97 us

profile of v2, /device:TPU:1, one launch (start us, length us, event | category | flops | bytes accessed | tf_op | source)
XLA Modules:
  0.0 29.3 jit_solution(14655300524814595497)
XLA Ops:
  0.0 28.3 %analysis.1 = bf16[8,4,64,256]{3,2,1,0:T(8,128)(2,1)S(1)} custom-call(bf16[8,4,64,256]{3,2,1,0:T(8,128)(2,1)} %state_ref.1, s32[1,256]{1,0:T(1,128)} %bitcast.3, f32[1,256]{1,0:T(1,128)} %bitcast.4, f32[1,256]{1,0:T(1,128)} %bitcast.5), custom_call_target="tpu_custom_call" | custom-call | tf_op jit(solution)/shard_map/analysis/pallas_call | solution.py:317
  28.3 1.0 %copy.6 = bf16[8,4,64,256]{3,2,1,0:T(8,128)(2,1)} copy(bf16[8,4,64,256]{3,2,1,0:T(8,128)(2,1)S(1)} %analysis.1) | data formatting | bytes 2097152
